TPU v7x, 256 devices: a whole 4x4x8 slice. The times are simulated.
256 devices in a mesh: grid: 128 (over x, z, y), rep: 2 (over core).
Axes of the slice: x: 4, y: 4, z: 8, core: 2. Of those that a mesh axis runs over, the one named last changes fastest.
Arguments:
- density_blocks: bfloat16 [3584, 4, 128, 128], P('grid'), may hold values from -0.046875 to 0.046875
- neighbours: int32 [3584, 4], P('grid'), may hold values from 0 to 3583, as said below
- relevant: int32 [3072, 8], P(('grid', 'rep')), may hold values from 0 to 3583, as said below
- batch_count: int32 [256], P(('grid', 'rep')), may hold values from 1 to 12, as said below
- basis_values: bfloat16 [3072, 8, 128, 128], P(('grid', 'rep')), may hold values from -6 to 6
- becke_weights: bfloat16 [3072, 128], P(('grid', 'rep')), may hold values from 0.0039978027 to 0.099609375
Outputs:
- xc_blocks: bfloat16 [3584, 4, 128, 128], P('grid')
Inputs may be any that keep to these rules, and one draw needn't show every extreme that they name: neighbours[a, 0] = a; the 4 column groups of a row group are distinct and lie within 12 consecutive groups that contain a. `relevant`: the 8 groups of a batch are distinct and lie within 12 consecutive groups around a group owned by the batch's grid index; none lies more than 6 groups before the first or after the last group owned by that grid index. `batch_count`: some device has all 12 slots live in every draw.
All inputs are finite; a program needn't handle non-finite values.
Results may differ from a plain program's by a relative error of at most 0.0049.
Values may be sent and summed in bfloat16 or wider, within the bound.
A program may use at most 192 MiB of HBM per device.

v0:
```python
import jax
import jax.numpy as jnp
from jax import lax
from jax.sharding import PartitionSpec as P

SPAN = 12


slater_coef = 0.9847450218426965


def shifted(block, axis, distance):
    devices = range(lax.axis_size(axis))
    route = [(i - distance, i) for i in devices if i - distance in devices]
    return lax.ppermute(block, axis, route)


def in_blocks(array, dim, count):
    before, after = (array.shape[:dim], array.shape[dim + 1 :])
    return jnp.moveaxis(array.reshape(*before, count, -1, *after), dim, 0)


def sum_at_owner(array, axis, dim):
    count = lax.axis_size(axis)
    pieces = lax.all_to_all(in_blocks(array, dim, count), axis, 0, 0, tiled=True)
    return jnp.sum(pieces, axis=0)


def potential(density_at):
    return -slater_coef * density_at * (density_at * density_at + 1.0) ** (-1.0 / 3.0)


def batch_terms(slabs, slab_neighbours, groups, basis_vals, weight_row):
    matches = (slab_neighbours[:, :, None] == groups[None, None, :]).astype(jnp.bfloat16)
    column_basis = jnp.einsum(
        "ikj,jnp->iknp", matches, basis_vals, preferred_element_type=jnp.float32
    ).astype(jnp.bfloat16)
    spread = jnp.einsum("ikmn,iknp->imp", slabs, column_basis, preferred_element_type=jnp.float32)
    basis_wide = basis_vals.astype(jnp.float32)
    density_at = jnp.sum(basis_wide * spread, axis=(0, 1))
    scaled = (
        basis_wide * (weight_row.astype(jnp.float32) * potential(density_at))[None, None, :]
    ).astype(jnp.bfloat16)
    column_scaled = jnp.einsum(
        "ikj,jnp->iknp", matches, scaled, preferred_element_type=jnp.float32
    ).astype(jnp.bfloat16)
    return jnp.einsum(
        "imp,iknp->ikmn", basis_vals, column_scaled, preferred_element_type=jnp.float32
    )


def shards(density_blocks, neighbours, relevant, batch_count, basis_values, becke_weights):
    group_count = density_blocks.shape[0]
    reach = SPAN // 2
    arrived = []
    for offset, low_edge in ((1, group_count - reach), (-1, 0)):
        arrived.append(
            shifted(
                (
                    density_blocks[low_edge : low_edge + reach],
                    neighbours[low_edge : low_edge + reach],
                ),
                "grid",
                offset,
            )
        )
    before_blocks, before_lists = arrived[0]
    after_blocks, after_lists = arrived[1]
    window_blocks = jnp.concatenate([before_blocks, density_blocks, after_blocks], axis=0)
    window_lists = jnp.concatenate([before_lists, neighbours, after_lists], axis=0)
    window_base = lax.axis_index("grid") * group_count - reach
    loop_count = batch_count[0]
    source_groups, source_basis, source_weights = (relevant, basis_values, becke_weights)

    def visit(step_index, buffer):
        groups = source_groups[step_index]
        local_rows = groups - window_base
        blocks = batch_terms(
            window_blocks[local_rows],
            window_lists[local_rows],
            groups,
            source_basis[step_index],
            source_weights[step_index],
        )
        return buffer.at[local_rows].add(blocks)

    start_buffer = jnp.zeros((group_count + 2 * reach,) + density_blocks.shape[1:], jnp.float32)
    buffer = lax.fori_loop(0, loop_count, visit, start_buffer)
    halves = sum_at_owner(buffer, "rep", 1)
    owned_half = halves[reach : reach + group_count]
    gained = []
    for offset, low_edge in ((1, reach + group_count), (-1, 0)):
        gained.append(shifted(halves[low_edge : low_edge + reach], "grid", offset))
    owned_half = owned_half.at[:reach].add(gained[0])
    owned_half = owned_half.at[group_count - reach :].add(gained[1])
    return lax.all_gather(owned_half.astype(jnp.bfloat16), "rep", axis=1, tiled=True)


def solution(mesh):
    placed = (
        P("grid", None, None, None),
        P("grid", None),
        P(("grid", "rep"), None),
        P(("grid", "rep")),
        P(("grid", "rep"), None, None, None),
        P(("grid", "rep"), None),
    )
    return jax.shard_map(
        shards, mesh=mesh, in_specs=placed, out_specs=P("grid", None, None, None), check_vma=False
    )
```

profile of v0, /device:TPU:3, one launch (start us, length us, event | category | flops | bytes accessed | tf_op | source)
XLA Modules:
  0.0 334.2 jit_solution(412478288045447949)
XLA Ops:
  6.5 0.0 all-gather.2.cloned.1.call-start
  6.5 2.4 fusion.26
  9.0 3.2 collective-permute-start.2
  12.2 8.6 %collective-permute-start.3 = (bf16[6,4,128,128]{3,2,1,0:T(8,128)(2,1)S(1)}, bf16[6,4,128,128]{3,2,1,0:T(8,128)(2,1)S(1)}, u32[]{:S(2)}, u32[]{:S(2)}) collective-permute-start(bf16[6,4,128,128]{3,2,1,0:T(8,128)(2,1)S(1)} %get-tuple-element.126), channel_id=1, source_target_pairs={{2,0},{4,2},{6,4},{8,6},{10,8},{12,10},{14,12},{16,14},{18,16},{20... | collective-permute-start | bytes 2359304 | tf_op jit(solution)/shard_map/ppermute | solution.py:15
  20.8 0.8 fusion.27
  21.6 1.9 collective-permute-start
  23.5 7.6 %collective-permute-start.1 = (s32[6,4]{0,1:T(4,128)S(1)}, s32[6,4]{0,1:T(4,128)S(1)}, u32[]{:S(2)}, u32[]{:S(2)}) collective-permute-start(s32[6,4]{0,1:T(4,128)S(1)} %get-tuple-element.128), channel_id=1, source_target_pairs={{2,0},{4,2},{6,4},{8,6},{10,8},{12,10},{14,12},{16,14},{18,16},{20... | collective-permute-start | bytes 296 | tf_op jit(solution)/shard_map/ppermute | solution.py:15
  31.1 0.8 copy.20
  31.9 4.4 %collective-permute-done = s32[6,4]{0,1:T(4,128)S(1)} collective-permute-done((s32[6,4]{0,1:T(4,128)S(1)}, s32[6,4]{0,1:T(4,128)S(1)}, u32[]{:S(2)}, u32[]{:S(2)}) %collective-permute-start) | collective-permute-done | bytes 128 | tf_op jit(solution)/shard_map/ppermute | solution.py:15
  36.4 0.7 collective-permute-done.1
  37.0 0.8 pad_add_fusion
  37.8 0.1 copy.21
  37.9 0.0 collective-permute-done.2
  37.9 0.0 collective-permute-done.3
  37.9 5.0 %pad_maximum_fusion = bf16[40,4,128,128]{3,2,1,0:T(8,128)(2,1)} fusion(bf16[6,4,128,128]{3,2,1,0:T(8,128)(2,1)S(1)} %collective-permute-done.3, bf16[28,4,128,128]{3,2,1,0:T(8,128)(2,1)} %param.12, bf16[6,4,128,128]{3,2,1,0:T(8,128)(2,1)S(1)} %collective-permute-done.2), kind=kLoop, calls=%fused_computation.37 | loop fusion | flops 5242880 | bytes 10485760 | tf_op jit(solution)/shard_map/concatenate | solution.py:69
  42.9 5.3 %broadcast_in_dim.2 = f32[40,4,128,128]{3,2,1,0:T(8,128)} broadcast(f32[]{:T(128)} %constant.81.clone.1), dimensions={} | broadcast | bytes 10485764 | tf_op jit(solution)/shard_map/broadcast_in_dim | solution.py:87
  48.2 17.1 %while.12 = (s32[]{:T(128)}, f32[40,4,128,128]{3,2,1,0:T(8,128)}, s32[]{:T(128)}, s32[12,8]{1,0:T(8,128)S(1)}, s32[]{:T(128)}, /*index=5*/s32[40,4]{1,0:T(8,128)...) while((s32[]{:T(128)}, f32[40,4,128,128]{3,2,1,0:T(8,128)}, ...), condition=%wide.region_3.0_spmd, body=%wide.region_0.0_spmd.sunk | while | flops 287574176 | bytes 23076084 | solution.py:88
  48.9 0.6 gather_fusion.1
  49.5 1.0 constant_dynamic-slice_fusion.4
  50.5 0.2 copy.61
  50.7 3.2 gather_fusion
  53.9 0.6 convolution_convert_fusion.4
  54.5 0.4 convolution_bitcast_fusion.4
  54.9 0.4 fusion.49
  55.3 0.7 fusion.50
  56.0 0.5 convolution_convert_fusion.5
  56.6 1.8 convolution_bitcast_fusion.5
  58.4 1.9 copy.62
  60.3 4.4 %scatter_fusion = f32[40,4,128,128]{3,2,1,0:T(8,128)} fusion(f32[40,4,128,128]{3,2,1,0:T(8,128)} %get-tuple-element.198, s32[8]{0:T(128)S(1)} %fusion.47, f32[8,4,128,128]{3,2,1,0:T(8,128)S(1)} %copy.62), kind=kCustom, calls=%fused_computation.2.clone.1 | custom fusion | flops 524288 | bytes 6291488 | tf_op jit(solution)/shard_map/while/body/scatter-add | solution.py:85
  65.4 4.8 %copy.23 = f32[2,40,2,128,128]{4,3,2,1,0:T(8,128)S(1)} copy(f32[2,40,2,128,128]{4,3,2,0,1:T(8,128)} %bitcast.73) | data formatting | bytes 20971520 | tf_op jit(solution)/shard_map/transpose | solution.py:20
  70.2 64.1 %all_to_all.5 = f32[2,40,2,128,128]{4,3,2,1,0:T(8,128)} all-to-all(f32[2,40,2,128,128]{4,3,2,1,0:T(8,128)S(1)} %copy.23), channel_id=1, replica_groups=mesh['grid'=128,'rep'=2] {'rep'}, dimensions={0} | all-to-all | bytes 20971520 | tf_op jit(solution)/shard_map/all_to_all | solution.py:25
  134.3 8.0 %reduce_sum.18 = f32[40,2,128,128]{3,2,1,0:T(8,128)} reduce(f32[2,40,2,128,128]{4,3,2,1,0:T(8,128)} %all_to_all.5, f32[]{:T(128)} %constant.81.clone.1), dimensions={0}, to_apply=%region_4.0 | reduce | flops 1310720 | bytes 15728644 | tf_op jit(solution)/shard_map/reduce_sum | solution.py:26
  142.3 0.0 copy-start
  142.3 1.7 fusion.25
  143.9 130.4 %collective-permute-start.4 = (f32[6,2,128,128]{3,2,1,0:T(8,128)S(1)}, f32[6,2,128,128]{3,2,1,0:T(8,128)S(1)}, u32[]{:S(2)}, u32[]{:S(2)}) collective-permute-start(f32[6,2,128,128]{3,2,1,0:T(8,128)S(1)} %get-tuple-element.124), channel_id=1, source_target_pairs={{0,2},{2,4},{4,6},{6,8},{8,10},{10,12},{12,14},{14,16},{16,18},{18... | collective-permute-start | bytes 2359304 | tf_op jit(solution)/shard_map/ppermute | solution.py:15
  274.3 0.0 slice-start
  274.3 2.2 collective-permute-start.5
  276.5 14.3 %collective-permute-done.4 = f32[6,2,128,128]{3,2,1,0:T(8,128)S(1)} collective-permute-done((f32[6,2,128,128]{3,2,1,0:T(8,128)S(1)}, f32[6,2,128,128]{3,2,1,0:T(8,128)S(1)}, u32[]{:S(2)}, u32[]{:S(2)}) %collective-permute-start.4) | collective-permute-done | bytes 786464 | tf_op jit(solution)/shard_map/ppermute | solution.py:15
  290.8 0.0 copy-done
  290.8 0.0 slice-done
  290.8 0.1 fusion.24
  290.9 4.0 %collective-permute-done.5 = f32[6,2,128,128]{3,2,1,0:T(8,128)S(1)} collective-permute-done((f32[6,2,128,128]{3,2,1,0:T(8,128)S(1)}, f32[6,2,128,128]{3,2,1,0:T(8,128)S(1)}, u32[]{:S(2)}, u32[]{:S(2)}) %collective-permute-start.5) | collective-permute-done | bytes 786464 | tf_op jit(solution)/shard_map/ppermute | solution.py:15
  294.9 0.2 fusion.23
  295.1 1.5 convert_element_type.26
  296.7 0.0 all-gather.2.cloned.1.call-update
  296.7 26.3 %all-gather.2.cloned.1.call-done = bf16[28,4,128,128]{3,2,1,0:T(8,128)(2,1)} async-done(((bf16[28,2,128,128]{3,2,1,0:T(8,128)(2,1)}), bf16[28,4,128,128]{3,2,1,0:T(8,128)(2,1)}) %all-gather.2.cloned.1.call-update) | async-done | bytes 3670032 | tf_op jit(solution)/shard_map/all_gather | solution.py:96
  323.0 4.4 %copy.73 = bf16[28,4,128,128]{3,2,1,0:T(8,128)(2,1)} copy(bf16[28,4,128,128]{3,2,1,0:T(8,128)(2,1)} %all-gather.2.cloned.1.call-done) | data formatting | bytes 7340032
  (3 shorter events, 0.0 us)
Async XLA Ops:
  6.5 316.5 %all-gather.2.cloned.1.call-start = ((), (), s32[]{:S(2)}) async-start(), calls=%async_computation.1 | async-start | bytes 5505024 | tf_op jit(solution)/shard_map/all_gather | solution.py:96
  9.0 28.9 %collective-permute-start.2 = (bf16[6,4,128,128]{3,2,1,0:T(8,128)(2,1)}, bf16[6,4,128,128]{3,2,1,0:T(8,128)(2,1)S(1)}, u32[]{:S(2)}, u32[]{:S(2)}) collective-permute-start(bf16[6,4,128,128]{3,2,1,0:T(8,128)(2,1)} %get-tuple-element.125), channel_id=1, source_target_pairs={{0,2},{2,4},{4,6},{6,8},{8,10},{10,12},{12,14},{14,16},{16,18},{18... | collective-permute-start | bytes 2359304 | tf_op jit(solution)/shard_map/ppermute | solution.py:15
  12.2 25.7 %collective-permute-start.3 = (bf16[6,4,128,128]{3,2,1,0:T(8,128)(2,1)S(1)}, bf16[6,4,128,128]{3,2,1,0:T(8,128)(2,1)S(1)}, u32[]{:S(2)}, u32[]{:S(2)}) collective-permute-start(bf16[6,4,128,128]{3,2,1,0:T(8,128)(2,1)S(1)} %get-tuple-element.126), channel_id=1, source_target_pairs={{2,0},{4,2},{6,4},{8,6},{10,8},{12,10},{14,12},{16,14},{18,16},{20... | collective-permute-start | bytes 2359304 | tf_op jit(solution)/shard_map/ppermute | solution.py:15
  21.6 14.7 %collective-permute-start = (s32[6,4]{0,1:T(4,128)S(1)}, s32[6,4]{0,1:T(4,128)S(1)}, u32[]{:S(2)}, u32[]{:S(2)}) collective-permute-start(s32[6,4]{0,1:T(4,128)S(1)} %get-tuple-element.127), channel_id=1, source_target_pairs={{0,2},{2,4},{4,6},{6,8},{8,10},{10,12},{12,14},{14,16},{16,18},{18... | collective-permute-start | bytes 296 | tf_op jit(solution)/shard_map/ppermute | solution.py:15
  23.5 13.5 %collective-permute-start.1 = (s32[6,4]{0,1:T(4,128)S(1)}, s32[6,4]{0,1:T(4,128)S(1)}, u32[]{:S(2)}, u32[]{:S(2)}) collective-permute-start(s32[6,4]{0,1:T(4,128)S(1)} %get-tuple-element.128), channel_id=1, source_target_pairs={{2,0},{4,2},{6,4},{8,6},{10,8},{12,10},{14,12},{16,14},{18,16},{20... | collective-permute-start | bytes 296 | tf_op jit(solution)/shard_map/ppermute | solution.py:15
  142.3 148.6 %copy-start = (f32[40,2,128,128]{3,2,1,0:T(8,128)S(1)}, f32[40,2,128,128]{3,2,1,0:T(8,128)}, u32[]{:S(2)}) copy-start(f32[40,2,128,128]{3,2,1,0:T(8,128)} %reduce_sum.18) | copy-start | bytes 15728644
  143.9 146.9 %collective-permute-start.4 = (f32[6,2,128,128]{3,2,1,0:T(8,128)S(1)}, f32[6,2,128,128]{3,2,1,0:T(8,128)S(1)}, u32[]{:S(2)}, u32[]{:S(2)}) collective-permute-start(f32[6,2,128,128]{3,2,1,0:T(8,128)S(1)} %get-tuple-element.124), channel_id=1, source_target_pairs={{0,2},{2,4},{4,6},{6,8},{8,10},{10,12},{12,14},{14,16},{16,18},{18... | collective-permute-start | bytes 2359304 | tf_op jit(solution)/shard_map/ppermute | solution.py:15
  274.3 16.5 %slice-start = ((f32[40,2,128,128]{3,2,1,0:T(8,128)}), f32[28,2,128,128]{3,2,1,0:T(8,128)S(1)}, s32[]{:S(2)}) async-start(f32[40,2,128,128]{3,2,1,0:T(8,128)} %reduce_sum.18), calls=%async_computation.2 | async-start | bytes 7340032 | tf_op jit(solution)/shard_map/slice | solution.py:90
  274.3 20.6 %collective-permute-start.5 = (f32[6,2,128,128]{3,2,1,0:T(8,128)S(1)}, f32[6,2,128,128]{3,2,1,0:T(8,128)S(1)}, u32[]{:S(2)}, u32[]{:S(2)}) collective-permute-start(f32[6,2,128,128]{3,2,1,0:T(8,128)S(1)} %get-tuple-element.123), channel_id=1, source_target_pairs={{2,0},{4,2},{6,4},{8,6},{10,8},{12,10},{14,12},{16,14},{18,16},{20... | collective-permute-start | bytes 2359304 | tf_op jit(solution)/shard_map/ppermute | solution.py:15
Sparse Core Ops, SparseCore 0:
  296.8 26.1 all-gather.1
where the time goes:
time: 337 us; the launch traced here: 334 us
  starting transfers between devices  154 us (46%)
  blocking collectives  64.1 us (19%)
  waiting for transfers between devices  49.8 us (15%)
  local copies, waits for them, and re-layouts  27.2 us (8%)
  other arithmetic  21.1 us (6%)
  between operations  13.5 us (4%)
    ppermute x6, starting transfers between devices, shifted(): return lax.ppermute(block, axis, route)  154 us
    all_to_all x1, blocking collectives, sum_at_owner(): lax.all_to_all(in_blocks(array, dim, count), axis, 0, 0, tiled=True)  64.1 us
    all_gather x1, waiting for transfers between devices, shards(): lax.all_gather(owned_half.astype(jnp.bfloat16), 'rep', axis=1, tiled=True)  26.3 us
    ppermute x6, waiting for transfers between devices, shifted(): return lax.ppermute(block, axis, route)  23.5 us
    reduce_sum x1, other arithmetic, sum_at_owner(): return jnp.sum(pieces, axis=0)  7.96 us
  transfers between devices with their start and end apart: 7, of which 5 were waited for; matrix products, arithmetic and copies ran while one was open for 1% of the time, Pallas kernels for 0%

commit v1 on v0

v1 whole, which is shorter than its diff:
```python
import jax
import jax.numpy as jnp
from jax import lax
from jax.experimental import pallas as pl
from jax.experimental.pallas import tpu as pltpu
from jax.sharding import PartitionSpec as P

SPAN = 12
REACH = SPAN // 2
MIB = 1 << 20
MESH = pl.DeviceIdType.MESH
F32 = jnp.float32
BF16 = jnp.bfloat16

slater_coef = 0.9847450218426965


def potential(density_at):
    softened = jnp.exp(jnp.log(density_at * density_at + 1.0) * (-1.0 / 3.0))
    return -slater_coef * density_at * softened


def surroundings():
    count = lax.axis_size("grid")
    here = lax.axis_index("grid")
    rep = lax.axis_index("rep")
    there = here + 2 * rep - 1
    faces = (there >= 0) & (there < count)
    facing = {"grid": jnp.clip(there, 0, count - 1), "rep": 1 - rep}
    return rep, faces, facing, {"rep": 1 - rep}


def announce(faces, facing, partner):
    barrier = pltpu.get_barrier_semaphore()

    @pl.when(faces)
    def _():
        pl.semaphore_signal(barrier, inc=1, device_id=facing, device_id_type=MESH)

    pl.semaphore_signal(barrier, inc=1, device_id=partner, device_id_type=MESH)


def gather_round(faces):
    pl.semaphore_wait(pltpu.get_barrier_semaphore(), 1 + faces.astype(jnp.int32))


def remote(source, target, send_sem, recv_sem, device):
    return pltpu.make_async_remote_copy(
        src_ref=source,
        dst_ref=target,
        send_sem=send_sem,
        recv_sem=recv_sem,
        device_id=device,
        device_id_type=MESH,
    )


def each(size, body):
    def step(index, carry):
        body(index)
        return carry

    lax.fori_loop(0, size, step, 0)


def in_vmem(array):
    return pltpu.with_memory_space_constraint(array, pltpu.VMEM)


def in_hbm(array):
    return pltpu.with_memory_space_constraint(array, pltpu.HBM)


def spread_density(own, values, picks, rows, b):
    r_groups = len(rows)
    density_at = jnp.zeros((8, values.shape[-1]), F32)
    for i in range(r_groups):
        spread = None
        for k in range(0, len(picks[i]), 2):
            left_side = jnp.concatenate([own[rows[i], k], own[rows[i], k + 1]], axis=1)
            right_side = jnp.concatenate(
                [values[b, picks[i][k]], values[b, picks[i][k + 1]]], axis=0
            )
            term = jnp.dot(left_side, right_side, preferred_element_type=F32)
            spread = term if spread is None else spread + term
        product = values[b, i].astype(F32) * spread
        density_at = density_at + jnp.sum(product.reshape(-1, 8, product.shape[-1]), axis=0)
    return density_at


def halo_kernel(
    relevant, list_scalars, lists, density, basis, halo, values, total, density_out, table_out,
    own, edge_lists, table, table_scalars, edge_scalars,
    local_sem, small_sem, send, recv, pass_send, pass_recv, list_send, list_recv, lists_on_send, lists_on_recv,
):
    rep, faces, facing, partner = surroundings()
    group_count, k_blocks = density.shape[:2]
    batch_total, r_groups = basis.shape[:2]
    base = lax.axis_index("grid") * group_count
    load_own = pltpu.make_async_copy(density, own, local_sem.at[0])
    load_values = pltpu.make_async_copy(
        basis, values.at[pl.ds(0, batch_total), pl.ds(0, r_groups)], local_sem.at[1]
    )
    announce(faces, facing, partner)
    load_own.start()
    load_values.start()

    lanes = table.shape[1]
    lane = lax.broadcasted_iota(jnp.int32, (1, lanes), 1)
    batch_of = lax.shift_right_logical(lane, 3)
    spot = lane & (r_groups - 1)
    slots = []
    for j in range(r_groups):
        held = jnp.full((1, lanes), -1, jnp.int32)
        for b in range(batch_total):
            held = jnp.where(batch_of == b, relevant[j, b], held)
        slots.append(held)
    mine = slots[0]
    for j in range(1, r_groups):
        mine = jnp.where(spot == j, slots[j], mine)
    local = mine - base
    columns = []
    for k in range(k_blocks):
        held = jnp.full((1, lanes), -1, jnp.int32)
        for row in range(group_count):
            held = jnp.where(local == row, list_scalars[k, row], held)
        columns.append(held)

    def write_table(columns, rows):
        for k in range(k_blocks):
            pick = jnp.full((1, lanes), r_groups, jnp.int32)
            for j in range(r_groups):
                pick = jnp.where(columns[k] == slots[j], j, pick)
            table[k : k + 1, :] = pick
        table[k_blocks : k_blocks + 1, :] = rows

    table[...] = jnp.zeros(table.shape, jnp.int32)
    write_table(columns, jnp.clip(local, 0, group_count - 1))
    to_scalars = pltpu.make_async_copy(table, table_scalars, small_sem.at[0])
    to_scalars.start()

    gather_round(faces)
    list_pass = remote(edge_lists.at[rep], edge_lists.at[rep], lists_on_send, lists_on_recv, partner)
    moves, passes = [], []
    for step in range(REACH):
        at = pl.ds(rep * REACH + step, 1)
        far = pl.ds((1 - rep) * REACH + step, 1)
        source = density.at[pl.ds(rep * (group_count - REACH) + step, 1)]
        moves.append(remote(source, halo.at[far], send.at[step], recv.at[step], facing))
        passes.append(remote(halo.at[at], halo.at[at], pass_send.at[step], pass_recv.at[step], partner))
    list_move = remote(lists, edge_lists.at[1 - rep], list_send, list_recv, facing)

    @pl.when(faces)
    def _():
        list_move.start()
        for move in moves:
            move.start()

    total[...] = jnp.zeros(total.shape, F32)

    def clear_blank(b):
        values[b, r_groups] = jnp.zeros(values.shape[2:], BF16)

    each(batch_total, clear_blank)
    to_scalars.wait()
    load_own.wait()
    load_values.wait()

    def one_batch(b):
        picks = [
            [table_scalars[k, b * r_groups + i] for k in range(k_blocks)] for i in range(r_groups)
        ]
        rows = [table_scalars[k_blocks, b * r_groups + i] for i in range(r_groups)]
        density_out[b] = spread_density(own, values, picks, rows, b)

    each(batch_total, one_batch)

    @pl.when(faces)
    def _():
        list_move.wait_recv()
        list_pass.start()
        for move, onward in zip(moves, passes):
            move.wait_recv()
            onward.start()

    count = lax.axis_size("grid")
    other = lax.axis_index("grid") + 1 - 2 * rep
    other_faces = (other >= 0) & (other < count)

    @pl.when(other_faces)
    def _():
        list_pass.wait_recv()

    @pl.when(faces)
    def _():
        list_pass.wait_send()

    @pl.when(jnp.logical_not(faces))
    def _():
        edge_lists[rep] = jnp.full(edge_lists.shape[1:], -1, jnp.int32)

    @pl.when(jnp.logical_not(other_faces))
    def _():
        edge_lists[1 - rep] = jnp.full(edge_lists.shape[1:], -1, jnp.int32)

    lists_down = pltpu.make_async_copy(edge_lists, edge_scalars, small_sem.at[0])
    lists_down.start()
    lists_down.wait()
    for k in range(k_blocks):
        held = columns[k]
        for step in range(REACH):
            below = group_count - REACH + step
            held = jnp.where(local == step - REACH, edge_scalars[0, k, below], held)
            held = jnp.where(local == group_count + step, edge_scalars[1, k, step], held)
        columns[k] = held
    write_table(columns, local + REACH)
    table_out[...] = table[...]

    @pl.when(other_faces)
    def _():
        for onward in passes:
            onward.wait_recv()

    @pl.when(faces)
    def _():
        list_move.wait_send()
        for move, onward in zip(moves, passes):
            move.wait_send()
            onward.wait_send()


def fetch_halo(relevant, lists, density_blocks, basis_values):
    group_count, k_blocks, side, _ = density_blocks.shape
    batch_total, r_groups = basis_values.shape[:2]
    rows = group_count + 2 * REACH
    scalars = pl.BlockSpec(memory_space=pltpu.SMEM)
    vector = pl.BlockSpec(memory_space=pltpu.VMEM)
    main = pl.BlockSpec(memory_space=pltpu.HBM)
    dma = pltpu.SemaphoreType.DMA
    return pl.pallas_call(
        halo_kernel,
        out_shape=(
            pltpu.VMEM((2 * REACH, k_blocks, side, side), BF16),
            pltpu.VMEM((batch_total, r_groups + 1, side, side), BF16),
            pltpu.VMEM((rows, k_blocks, side, side), F32),
            pltpu.VMEM((batch_total, 8, side), F32),
            pltpu.VMEM((8, 128), jnp.int32),
        ),
        in_specs=[scalars, scalars, vector, main, main],
        out_specs=(vector,) * 5,
        scratch_shapes=[
            pltpu.VMEM((group_count, k_blocks, side, side), BF16),
            pltpu.VMEM((2,) + lists.shape, jnp.int32),
            pltpu.VMEM((8, 128), jnp.int32),
            pltpu.SMEM((8, 128), jnp.int32),
            pltpu.SMEM((2,) + lists.shape, jnp.int32),
            dma((2,)),
            dma((1,)),
            dma((REACH,)),
            dma((REACH,)),
            dma((REACH,)),
            dma((REACH,)),
            dma,
            dma,
            dma,
            dma,
        ],
        compiler_params=pltpu.CompilerParams(
            collective_id=0, has_side_effects=True, vmem_limit_bytes=8 * MIB
        ),
        name="halo",
    )(relevant, lists, lists, in_hbm(density_blocks), in_hbm(basis_values))


def batch_kernel(
    live, table, weights, halo, values, density_own, start, total,
    scaled_even, scaled_odd, density_at, factor, edge_list,
):
    del start
    batch_total, pages = values.shape[:2]
    r_groups = pages - 1
    k_blocks = total.shape[1]
    owned_end = total.shape[0] - REACH
    count = live[0]
    for scaled in (scaled_even, scaled_odd):
        scaled[r_groups] = jnp.zeros(total.shape[2:], BF16)
    density_at[...] = density_own[...]

    def collect(b, found):
        for i in range(r_groups):
            code = b * r_groups + i
            row = table[k_blocks, code]
            edge_list[found] = code
            outside = (row < REACH) | (row >= owned_end)
            found = found + outside.astype(jnp.int32)
        return found

    found = lax.fori_loop(0, count, collect, 0)
    edge_list[found] = 0

    def add_edges(step, carry):
        pieces = []
        for part in range(2):
            index = 2 * step + part
            code = edge_list[index]
            b = lax.shift_right_logical(code, 3)
            row = table[k_blocks, code]
            row = jnp.clip(jnp.where(row < REACH, row, row - owned_end + REACH), 0, 2 * REACH - 1)
            picks = [jnp.where(index < found, table[k, code], r_groups) for k in range(k_blocks)]
            spread = None
            for k in range(0, k_blocks, 2):
                left_side = jnp.concatenate([halo[row, k], halo[row, k + 1]], axis=1)
                right_side = jnp.concatenate([values[b, picks[k]], values[b, picks[k + 1]]], axis=0)
                term = jnp.dot(left_side, right_side, preferred_element_type=F32)
                spread = term if spread is None else spread + term
            product = values[b, code & (r_groups - 1)].astype(F32) * spread
            pieces.append((b, jnp.sum(product.reshape(-1, 8, product.shape[-1]), axis=0)))
        for b, piece in pieces:
            density_at[b] += piece
        return carry

    lax.fori_loop(0, lax.shift_right_logical(found + 1, 1), add_edges, 0)
    factor[...] = weights[...].astype(F32) * potential(jnp.sum(density_at[...], axis=1))

    def scale(b, scaled):
        row = factor[pl.ds(b, 1), :]
        for i in range(r_groups):
            scaled[i] = (values[b, i].astype(F32) * row).astype(BF16)

    def add_terms(b, scaled):
        for i in range(r_groups):
            code = b * r_groups + i
            row = table[k_blocks, code]
            for k in range(0, k_blocks, 2):
                columns = jnp.concatenate(
                    [scaled[table[k, code]], scaled[table[k + 1, code]]], axis=0
                )
                terms = lax.dot_general(
                    values[b, i], columns, (((1,), (1,)), ((), ())), preferred_element_type=F32
                )
                side = terms.shape[0]
                total[row, k] += terms[:, :side]
                total[row, k + 1] += terms[:, side:]

    def two(step, carry):
        scale(2 * step, scaled_even)
        scale(2 * step + 1, scaled_odd)
        add_terms(2 * step, scaled_even)
        add_terms(2 * step + 1, scaled_odd)
        return carry

    lax.fori_loop(0, lax.shift_right_logical(count, 1), two, 0)

    @pl.when((count & 1) == 1)
    def _():
        scale(count - 1, scaled_even)
        add_terms(count - 1, scaled_even)


def block_sums(batch_count, fetched, becke_weights):
    halo, values, start, density_own, table = fetched
    batch_total, pages, side, _ = values.shape
    scalars = pl.BlockSpec(memory_space=pltpu.SMEM)
    vector = pl.BlockSpec(memory_space=pltpu.VMEM)
    return pl.pallas_call(
        batch_kernel,
        out_shape=pltpu.VMEM(start.shape, F32),
        in_specs=[scalars] * 2 + [vector] * 5,
        out_specs=vector,
        input_output_aliases={6: 0},
        scratch_shapes=[
            pltpu.VMEM((pages, side, side), BF16),
            pltpu.VMEM((pages, side, side), BF16),
            pltpu.VMEM(density_own.shape, F32),
            pltpu.VMEM((batch_total, side), F32),
            pltpu.SMEM((128,), jnp.int32),
        ],
        compiler_params=pltpu.CompilerParams(vmem_limit_bytes=4 * MIB),
        name="batches",
    )(
        batch_count, table, becke_weights,
        in_vmem(halo), in_vmem(values), in_vmem(density_own), in_vmem(start),
    )


def reduce_kernel(
    total, out, sent, got, edge_out, edge_in,
    swap_send, swap_recv, edge_send, edge_recv, done_send, done_recv,
):
    rep, faces, facing, partner = surroundings()
    group_count = out.shape[0]
    inner = (group_count - 2 * REACH) // 2
    announce(faces, facing, partner)

    def halo_at(which):
        return which * (group_count + REACH)

    def edge_at(which):
        return REACH + which * (group_count - REACH)

    def inner_at(which):
        return 2 * REACH + which * inner

    def pack(first, at, size):
        def step(row):
            sent[at + row] = total[first + row].astype(BF16)

        each(size, step)

    swaps = []

    def swap(at, size):
        index = len(swaps)
        rows_at = pl.ds(at, size)
        copy = remote(
            sent.at[rows_at], got.at[rows_at], swap_send.at[index], swap_recv.at[index], partner
        )
        copy.start()
        swaps.append(copy)

    pack(halo_at(1 - rep), 0, REACH)
    gather_round(faces)
    for step in range(REACH):
        swap(step, 1)
    pack(inner_at(1 - rep), 2 * REACH, inner)
    swap(2 * REACH, inner)
    pack(edge_at(1 - rep), REACH, REACH)
    swap(REACH, REACH)

    edges = []
    for step in range(REACH):
        swaps[step].wait_recv()
        edge_out[step] = (total[halo_at(rep) + step] + got[step].astype(F32)).astype(BF16)
        edge = remote(edge_out.at[step], edge_in.at[step], edge_send.at[step], edge_recv.at[step], facing)
        edges.append(edge)

        @pl.when(faces)
        def _():
            edge.start()

    finals = []

    def hand_over(first, size):
        index = len(finals)
        rows_at = pl.ds(first, size)
        copy = remote(
            out.at[rows_at], out.at[rows_at], done_send.at[index], done_recv.at[index], partner
        )
        copy.start()
        finals.append(copy)

    swaps[REACH].wait_recv()
    first_inner = inner_at(rep)

    def add_inner(row):
        out[first_inner - REACH + row] = (
            total[first_inner + row] + got[2 * REACH + row].astype(F32)
        ).astype(BF16)

    each(inner, add_inner)
    hand_over(first_inner - REACH, inner)

    swaps[REACH + 1].wait_recv()
    for step in range(REACH):
        row = edge_at(rep) + step

        @pl.when(faces)
        def _():
            edges[step].wait_recv()
            out[row - REACH] = (
                total[row] + got[REACH + step].astype(F32) + edge_in[step].astype(F32)
            ).astype(BF16)

        @pl.when(jnp.logical_not(faces))
        def _():
            out[row - REACH] = (total[row] + got[REACH + step].astype(F32)).astype(BF16)

        hand_over(row - REACH, 1)

    @pl.when(faces)
    def _():
        for edge in edges:
            edge.wait_send()

    for copy in swaps:
        copy.wait_send()
    for copy in finals:
        copy.wait()


def reduced(total, group_count):
    rows, k_blocks, side, _ = total.shape
    half_rows = rows // 2
    vector = pl.BlockSpec(memory_space=pltpu.VMEM)
    dma = pltpu.SemaphoreType.DMA
    return pl.pallas_call(
        reduce_kernel,
        out_shape=pltpu.VMEM((group_count, k_blocks, side, side), BF16),
        in_specs=[vector],
        out_specs=vector,
        scratch_shapes=[
            pltpu.VMEM((half_rows, k_blocks, side, side), BF16),
            pltpu.VMEM((half_rows, k_blocks, side, side), BF16),
            pltpu.VMEM((REACH, k_blocks, side, side), BF16),
            pltpu.VMEM((REACH, k_blocks, side, side), BF16),
            dma((REACH + 2,)),
            dma((REACH + 2,)),
            dma((REACH,)),
            dma((REACH,)),
            dma((REACH + 1,)),
            dma((REACH + 1,)),
        ],
        compiler_params=pltpu.CompilerParams(
            collective_id=1, has_side_effects=True, vmem_limit_bytes=12 * MIB
        ),
        name="reduce",
    )(in_vmem(total))


def shards(density_blocks, neighbours, relevant, batch_count, basis_values, becke_weights):
    fetched = fetch_halo(relevant.T, neighbours.T, density_blocks, basis_values)
    total = block_sums(batch_count, fetched, becke_weights)
    return reduced(total, density_blocks.shape[0])


def solution(mesh):
    placed = (
        P("grid", None, None, None),
        P("grid", None),
        P(("grid", "rep"), None),
        P(("grid", "rep")),
        P(("grid", "rep"), None, None, None),
        P(("grid", "rep"), None),
    )
    return jax.shard_map(
        shards, mesh=mesh, in_specs=placed, out_specs=P("grid", None, None, None), check_vma=False
    )
```

time: 337 us -> 50.3 us (0.15)
  starting transfers between devices: 154 us -> 0 us
  blocking collectives: 64.1 us -> 0 us
  waiting for transfers between devices: 49.8 us -> 0 us
  Pallas kernels: 0 us -> 46.5 us
  local copies, waits for them, and re-layouts: 27.2 us -> 3.2 us
  other arithmetic: 21.1 us -> 0 us
  between operations: 13.5 us -> 0.71 us
    ppermute x6 -> x0, starting transfers between devices: 154 us -> none  [shifted(): return lax.ppermute(block, axis, route)]
    all_to_all x1 -> x0, blocking collectives: 64.1 us -> none  [sum_at_owner(): lax.all_to_all(in_blocks(array, dim, count), axis, 0, 0, tiled=True)]
    pallas_call x0 -> x3, Pallas kernels: none -> 46.5 us  [the longest x1 24.5 us: reduced(): pl.pallas_call(reduce_kernel, out_shape=pltpu.VMEM((group_count, k_blocks...]
    all_gather x1 -> x0, waiting for transfers between devices: 26.3 us -> none  [shards(): lax.all_gather(owned_half.astype(jnp.bfloat16), 'rep', axis=1, tiled=True)]
    ppermute x6 -> x0, waiting for transfers between devices: 23.5 us -> none  [shifted(): return lax.ppermute(block, axis, route)]
    reduce_sum x2 -> x0, other arithmetic: 8.38 us -> none  [the longest x1 7.96 us: sum_at_owner(): return jnp.sum(pieces, axis=0)]
    transpose x2 -> x0, local copies, waits for them, and re-layouts: 6.75 us -> none  [the longest x1 4.83 us: in_blocks(): return jnp.moveaxis(array.reshape(*before, count, -1, *after), dim, 0)]
    concatenate x2 -> x0, other arithmetic: 5.79 us -> none  [the longest x1 5.03 us: shards(): jnp.concatenate([before_blocks, density_blocks, after_blocks], axis=0)]
  transfers between devices with their start and end apart: 7 -> 0, of which waited for: 5 -> 0; matrix products, arithmetic and copies ran while one was open for 1% -> 0% of each run, Pallas kernels for 0% -> 0%
where the time goes in v1:
time: 50.3 us; the launch traced here: 50.4 us
  Pallas kernels  46.5 us (92%)
  local copies, waits for them, and re-layouts  3.2 us (6%)
  between operations  0.71 us (1%)
    pallas_call x1, Pallas kernels, reduced(): pl.pallas_call(reduce_kernel, out_shape=pltpu.VMEM((group_count, k_blocks...  24.5 us
    pallas_call x1, Pallas kernels, fetch_halo(): pl.pallas_call(halo_kernel, out_shape=(pltpu.VMEM((2 * REACH, k_blocks, s...  20.7 us
    unnamed x7, local copies, waits for them, and re-layouts  3.2 us
    pallas_call x1, Pallas kernels, block_sums(): pl.pallas_call(batch_kernel, out_shape=pltpu.VMEM(start.shape, F32), in_s...  1.2 us

profile of v1, /device:TPU:3, one launch (start us, length us, event | category | flops | bytes accessed | tf_op | source)
XLA Modules:
  0.0 50.4 jit_solution(6402522427809567714)
XLA Ops:
  0.0 0.0 copy-start.1
  0.7 0.0 copy-start
  0.7 0.7 %copy-done = s32[28,4]{0,1:T(4,128)S(1)} copy-done((s32[28,4]{0,1:T(4,128)S(1)}, s32[28,4]{0,1:T(4,128)}, u32[]{:S(2)}) %copy-start) | copy-done | bytes 472
  1.4 0.0 copy-start.2
  1.4 0.7 %copy-done.2 = s32[12,8]{0,1:T(8,128)S(1)} copy-done((s32[12,8]{0,1:T(8,128)S(1)}, s32[12,8]{0,1:T(8,128)}, u32[]{:S(2)}) %copy-start.2) | copy-done | bytes 408
  2.0 20.7 %halo.1 = (bf16[12,4,128,128]{3,2,1,0:T(8,128)(2,1)S(1)}, bf16[12,9,128,128]{3,2,1,0:T(8,128)(2,1)S(1)}, f32[40,4,128,128]{3,2,1,0:T(8,128)S(1)}, f32[12,8,128]{2,1,0:T(8,128)S(1)}, s32[8,128]{1,0:T(8,128)S(1)}) custom-call(s32[8,12]{1,0:T(8,128)S(1)} %bitcast.4, s32[4,28]{1,0:T(4,128)S(1)} %bitcast.2, s32[4,28]{1,0:T(4,128)S(1)} %bitcast.3, ...), custom_call_target="tpu_custom_call" | custom-call | tf_op jit(solution)/shard_map/halo/pallas_call | solution.py:240
  22.8 0.0 copy-done.1
  22.8 1.2 %batches.1.total = f32[40,4,128,128]{3,2,1,0:T(8,128)S(1)} custom-call(s32[1]{0:T(128)S(6)} %copy.11.live, s32[8,128]{1,0:T(8,128)S(1)} %get-tuple-element.10.table, bf16[12,128]{1,0:T(8,128)(2,1)S(1)} %copy-done.1, bf16[12,4,128,128]{3,2,1,0:T(8,128)(2,1)S(1)} %get-tuple-element.11.halo, ...), custom_call_target="tpu_custom_call", output_to_operand_aliasing={{}: (6, {})} | custom-call | tf_op jit(solution)/shard_map/batches/pallas_call | solution.py:365
  24.0 24.5 %reduce.1 = bf16[28,4,128,128]{3,2,1,0:T(8,128)(2,1)S(1)} custom-call(f32[40,4,128,128]{3,2,1,0:T(8,128)S(1)} %batches.1.total), custom_call_target="tpu_custom_call" | custom-call | tf_op jit(solution)/shard_map/reduce/pallas_call | solution.py:496
  48.5 1.8 %copy.10 = bf16[28,4,128,128]{3,2,1,0:T(8,128)(2,1)} copy(bf16[28,4,128,128]{3,2,1,0:T(8,128)(2,1)S(1)} %reduce.1) | data formatting | bytes 7340032
Async XLA Ops:
  0.0 22.8 %copy-start.1 = (bf16[12,128]{1,0:T(8,128)(2,1)S(1)}, bf16[12,128]{1,0:T(8,128)(2,1)}, u32[]{:S(2)}) copy-start(bf16[12,128]{1,0:T(8,128)(2,1)} %weights.1) | copy-start | bytes 9220
  0.7 0.7 %copy-start = (s32[28,4]{0,1:T(4,128)S(1)}, s32[28,4]{0,1:T(4,128)}, u32[]{:S(2)}) copy-start(s32[28,4]{0,1:T(4,128)} %param.7) | copy-start | bytes 1348
  1.4 0.7 %copy-start.2 = (s32[12,8]{0,1:T(8,128)S(1)}, s32[12,8]{0,1:T(8,128)}, u32[]{:S(2)}) copy-start(s32[12,8]{0,1:T(8,128)} %param.8) | copy-start | bytes 1156

commit v2 on v1

v2 whole, which is shorter than its diff:
```python
import functools

import jax
import jax.numpy as jnp
from jax import lax
from jax.experimental import pallas as pl
from jax.experimental.pallas import tpu as pltpu
from jax.sharding import PartitionSpec as P

SPAN = 12
REACH = SPAN // 2
MIB = 1 << 20
MESH = pl.DeviceIdType.MESH
F32 = jnp.float32
BF16 = jnp.bfloat16

slater_coef = 0.9847450218426965


def potential(density_at):
    softened = jnp.exp(jnp.log(density_at * density_at + 1.0) * (-1.0 / 3.0))
    return -slater_coef * density_at * softened


def surroundings():
    count = lax.axis_size("grid")
    here = lax.axis_index("grid")
    rep = lax.axis_index("rep")
    there = here + 2 * rep - 1
    faces = (there >= 0) & (there < count)
    facing = {"grid": jnp.clip(there, 0, count - 1), "rep": 1 - rep}
    return rep, faces, facing, {"rep": 1 - rep}


def announce(faces, facing, partner):
    barrier = pltpu.get_barrier_semaphore()

    @pl.when(faces)
    def _():
        pl.semaphore_signal(barrier, inc=1, device_id=facing, device_id_type=MESH)

    pl.semaphore_signal(barrier, inc=1, device_id=partner, device_id_type=MESH)


def gather_round(faces):
    pl.semaphore_wait(pltpu.get_barrier_semaphore(), 1 + faces.astype(jnp.int32))


def remote(source, target, send_sem, recv_sem, device):
    return pltpu.make_async_remote_copy(
        src_ref=source,
        dst_ref=target,
        send_sem=send_sem,
        recv_sem=recv_sem,
        device_id=device,
        device_id_type=MESH,
    )


def each(size, body):
    def step(index, carry):
        body(index)
        return carry

    lax.fori_loop(0, size, step, 0)


def in_vmem(array):
    return pltpu.with_memory_space_constraint(array, pltpu.VMEM)


def in_hbm(array):
    return pltpu.with_memory_space_constraint(array, pltpu.HBM)


def spread_density(own, values, picks, rows, b):
    r_groups = len(rows)
    density_at = jnp.zeros((8, values.shape[-1]), F32)
    for i in range(r_groups):
        spread = None
        for k in range(0, len(picks[i]), 2):
            left_side = jnp.concatenate([own[rows[i], k], own[rows[i], k + 1]], axis=1)
            right_side = jnp.concatenate(
                [values[b, picks[i][k]], values[b, picks[i][k + 1]]], axis=0
            )
            term = jnp.dot(left_side, right_side, preferred_element_type=F32)
            spread = term if spread is None else spread + term
        product = values[b, i].astype(F32) * spread
        density_at = density_at + jnp.sum(product.reshape(-1, 8, product.shape[-1]), axis=0)
    return density_at


def halo_kernel(
    relevant, lists, density, basis, halo, values, edge_total, density_out, table_out, sources,
    own, edge_lists, table, relevant_rows, relevant_scalars, list_scalars, table_scalars, edge_scalars,
    local_sem, small_sem, send, recv, pass_send, pass_recv, list_send, list_recv, lists_on_send, lists_on_recv,
):
    rep, faces, facing, partner = surroundings()
    group_count, k_blocks = density.shape[:2]
    batch_total, r_groups = basis.shape[:2]
    base = lax.axis_index("grid") * group_count
    announce(faces, facing, partner)
    small = [
        pltpu.make_async_copy(relevant, relevant_scalars, small_sem.at[0]),
        pltpu.make_async_copy(lists, list_scalars, small_sem.at[1]),
        pltpu.make_async_copy(relevant, relevant_rows, small_sem.at[2]),
    ]
    load_own = pltpu.make_async_copy(density, own, local_sem.at[0])
    load_values = pltpu.make_async_copy(
        basis, values.at[pl.ds(0, batch_total), pl.ds(0, r_groups)], local_sem.at[1]
    )
    for copy in small:
        copy.start()
    load_own.start()
    load_values.start()
    list_move = remote(lists, edge_lists.at[1 - rep], list_send, list_recv, facing)
    list_pass = remote(edge_lists.at[rep], edge_lists.at[rep], lists_on_send, lists_on_recv, partner)
    moves, passes = [], []
    for step in range(REACH):
        at = pl.ds(rep * REACH + step, 1)
        far = pl.ds((1 - rep) * REACH + step, 1)
        source = density.at[pl.ds(rep * (group_count - REACH) + step, 1)]
        moves.append(remote(source, halo.at[far], send.at[step], recv.at[step], facing))
        passes.append(remote(halo.at[at], halo.at[at], pass_send.at[step], pass_recv.at[step], partner))
    gather_round(faces)

    @pl.when(faces)
    def _():
        list_move.start()
        for move in moves:
            move.start()

    for copy in small:
        copy.wait()

    lanes = table.shape[1]
    lane = lax.broadcasted_iota(jnp.int32, (1, lanes), 1)
    batch_of = lax.shift_right_logical(lane, 3)
    spot = lane & (r_groups - 1)
    slots = []
    for j in range(r_groups):
        held = jnp.full((1, lanes), -1, jnp.int32)
        for b in range(batch_total):
            held = jnp.where(batch_of == b, relevant_scalars[j, b], held)
        slots.append(held)
    mine = slots[0]
    for j in range(1, r_groups):
        mine = jnp.where(spot == j, slots[j], mine)
    local = mine - base
    columns = []
    for k in range(k_blocks):
        held = jnp.full((1, lanes), -1, jnp.int32)
        for row in range(group_count):
            held = jnp.where(local == row, list_scalars[k, row], held)
        columns.append(held)

    def write_table(columns, rows):
        for k in range(k_blocks):
            pick = jnp.full((1, lanes), r_groups, jnp.int32)
            for j in range(r_groups):
                pick = jnp.where(columns[k] == slots[j], j, pick)
            table[k : k + 1, :] = pick
        table[k_blocks : k_blocks + 1, :] = rows

    table[...] = jnp.zeros(table.shape, jnp.int32)
    write_table(columns, jnp.clip(local, 0, group_count - 1))
    to_scalars = pltpu.make_async_copy(table, table_scalars, small_sem.at[0])
    to_scalars.start()

    owned_row = lax.broadcasted_iota(jnp.int32, sources.shape, 0)
    batch = lax.broadcasted_iota(jnp.int32, sources.shape, 1)
    found = jnp.full(sources.shape, batch_total * r_groups, jnp.int32)
    for j in range(r_groups):
        hit = relevant_rows[j : j + 1, :] - base == owned_row
        found = jnp.where(hit, batch * r_groups + j, found)
    sources[...] = found

    edge_total[...] = jnp.zeros(edge_total.shape, F32)

    def clear_blank(b):
        values[b, r_groups] = jnp.zeros(values.shape[2:], BF16)

    each(batch_total, clear_blank)
    to_scalars.wait()
    load_own.wait()
    load_values.wait()

    def one_batch(b):
        picks = [
            [table_scalars[k, b * r_groups + i] for k in range(k_blocks)] for i in range(r_groups)
        ]
        rows = [table_scalars[k_blocks, b * r_groups + i] for i in range(r_groups)]
        density_out[b] = spread_density(own, values, picks, rows, b)

    each(batch_total, one_batch)

    @pl.when(faces)
    def _():
        list_move.wait_recv()
        list_pass.start()
        for move, onward in zip(moves, passes):
            move.wait_recv()
            onward.start()

    count = lax.axis_size("grid")
    other = lax.axis_index("grid") + 1 - 2 * rep
    other_faces = (other >= 0) & (other < count)

    @pl.when(other_faces)
    def _():
        list_pass.wait_recv()

    @pl.when(faces)
    def _():
        list_pass.wait_send()

    @pl.when(jnp.logical_not(faces))
    def _():
        edge_lists[rep] = jnp.full(edge_lists.shape[1:], -1, jnp.int32)

    @pl.when(jnp.logical_not(other_faces))
    def _():
        edge_lists[1 - rep] = jnp.full(edge_lists.shape[1:], -1, jnp.int32)

    lists_down = pltpu.make_async_copy(edge_lists, edge_scalars, small_sem.at[1])
    lists_down.start()
    lists_down.wait()
    for k in range(k_blocks):
        held = columns[k]
        for step in range(REACH):
            below = group_count - REACH + step
            held = jnp.where(local == step - REACH, edge_scalars[0, k, below], held)
            held = jnp.where(local == group_count + step, edge_scalars[1, k, step], held)
        columns[k] = held
    write_table(columns, local + REACH)
    table_out[...] = table[...]

    @pl.when(other_faces)
    def _():
        for onward in passes:
            onward.wait_recv()

    @pl.when(faces)
    def _():
        list_move.wait_send()
        for move, onward in zip(moves, passes):
            move.wait_send()
            onward.wait_send()


def fetch_halo(relevant, lists, density_blocks, basis_values):
    group_count, k_blocks, side, _ = density_blocks.shape
    batch_total, r_groups = basis_values.shape[:2]
    vector = pl.BlockSpec(memory_space=pltpu.VMEM)
    main = pl.BlockSpec(memory_space=pltpu.HBM)
    dma = pltpu.SemaphoreType.DMA
    return pl.pallas_call(
        halo_kernel,
        out_shape=(
            pltpu.VMEM((2 * REACH, k_blocks, side, side), BF16),
            pltpu.VMEM((batch_total, r_groups + 1, side, side), BF16),
            pltpu.VMEM((2 * REACH, k_blocks, side, side), F32),
            pltpu.VMEM((batch_total, 8, side), F32),
            pltpu.VMEM((8, 128), jnp.int32),
            pltpu.VMEM((group_count, batch_total), jnp.int32),
        ),
        in_specs=[main] * 4,
        out_specs=(vector,) * 6,
        scratch_shapes=[
            pltpu.VMEM((group_count, k_blocks, side, side), BF16),
            pltpu.VMEM((2,) + lists.shape, jnp.int32),
            pltpu.VMEM((8, 128), jnp.int32),
            pltpu.VMEM(relevant.shape, jnp.int32),
            pltpu.SMEM(relevant.shape, jnp.int32),
            pltpu.SMEM(lists.shape, jnp.int32),
            pltpu.SMEM((8, 128), jnp.int32),
            pltpu.SMEM((2,) + lists.shape, jnp.int32),
            dma((2,)),
            dma((3,)),
            dma((REACH,)),
            dma((REACH,)),
            dma((REACH,)),
            dma((REACH,)),
            dma,
            dma,
            dma,
            dma,
        ],
        compiler_params=pltpu.CompilerParams(
            collective_id=0, has_side_effects=True, vmem_limit_bytes=8 * MIB
        ),
        name="halo",
    )(in_hbm(relevant), in_hbm(lists), in_hbm(density_blocks), in_hbm(basis_values))


def edge_kernel(
    group_count, live, table, weights, halo, values, density_own, start, edge_total, factor, density_at, edge_list,
):
    del start
    batch_total, pages = values.shape[:2]
    r_groups = pages - 1
    k_blocks = halo.shape[1]
    owned_end = REACH + group_count
    count = live[0]
    density_at[...] = density_own[...]

    def collect(b, found):
        for i in range(r_groups):
            code = b * r_groups + i
            row = table[k_blocks, code]
            edge_list[found] = code
            outside = (row < REACH) | (row >= owned_end)
            found = found + outside.astype(jnp.int32)
        return found

    found = lax.fori_loop(0, count, collect, 0)
    edge_list[found] = 0

    def entry(index):
        code = edge_list[index]
        row = table[k_blocks, code]
        row = jnp.clip(jnp.where(row < REACH, row, row - owned_end + REACH), 0, 2 * REACH - 1)
        picks = [jnp.where(index < found, table[k, code], r_groups) for k in range(k_blocks)]
        return lax.shift_right_logical(code, 3), code & (r_groups - 1), row, picks

    def two_of(body):
        def step(index, carry):
            body([entry(2 * index), entry(2 * index + 1)])
            return carry

        lax.fori_loop(0, lax.shift_right_logical(found + 1, 1), step, 0)

    def add_density(entries):
        parts = []
        for b, i, row, picks in entries:
            spread = None
            for k in range(0, k_blocks, 2):
                left_side = jnp.concatenate([halo[row, k], halo[row, k + 1]], axis=1)
                right_side = jnp.concatenate([values[b, picks[k]], values[b, picks[k + 1]]], axis=0)
                term = jnp.dot(left_side, right_side, preferred_element_type=F32)
                spread = term if spread is None else spread + term
            product = values[b, i].astype(F32) * spread
            parts.append(jnp.sum(product.reshape(-1, 8, product.shape[-1]), axis=0))
        for (b, _, _, _), part in zip(entries, parts):
            density_at[b] += part

    two_of(add_density)
    factors = weights[...].astype(F32) * potential(jnp.sum(density_at[...], axis=1))
    slot = lax.broadcasted_iota(jnp.int32, factors.shape, 0)
    factor[...] = jnp.where(slot < count, factors, 0.0)

    def add_terms(entries):
        terms = []
        for b, i, row, picks in entries:
            factor_row = factor[pl.ds(b, 1), :]
            for k in range(0, k_blocks, 2):
                columns = jnp.concatenate(
                    [(values[b, picks[k + n]].astype(F32) * factor_row).astype(BF16) for n in range(2)],
                    axis=0,
                )
                terms.append(
                    lax.dot_general(
                        values[b, i], columns, (((1,), (1,)), ((), ())), preferred_element_type=F32
                    )
                )
        side = halo.shape[-1]
        for (_, _, row, _), pair in zip(entries, (terms[: len(terms) // 2], terms[len(terms) // 2 :])):
            for k in range(k_blocks):
                edge_total[row, k] += pair[k // 2][:, side * (k % 2) : side * (k % 2 + 1)]

    two_of(add_terms)


def edge_sums(batch_count, fetched, becke_weights, group_count):
    halo, values, start, density_own, table, _ = fetched
    batch_total, _, side, _ = values.shape
    scalars = pl.BlockSpec(memory_space=pltpu.SMEM)
    vector = pl.BlockSpec(memory_space=pltpu.VMEM)
    return pl.pallas_call(
        functools.partial(edge_kernel, group_count),
        out_shape=(pltpu.VMEM(start.shape, F32), pltpu.VMEM((batch_total, side), F32)),
        in_specs=[scalars] * 2 + [vector] * 5,
        out_specs=(vector, vector),
        input_output_aliases={6: 0},
        scratch_shapes=[
            pltpu.VMEM(density_own.shape, F32),
            pltpu.SMEM((128,), jnp.int32),
        ],
        compiler_params=pltpu.CompilerParams(vmem_limit_bytes=4 * MIB),
        name="edges",
    )(
        batch_count, table, becke_weights,
        in_vmem(halo), in_vmem(values), in_vmem(density_own), in_vmem(start),
    )


def reduce_kernel(
    edge_total, values, factor, table, sources, out,
    table_scalars, source_scalars, terms, scaled_even, scaled_odd, sent, got, owned, edge_out, edge_in,
    small_sem, swap_send, swap_recv, edge_send, edge_recv, done_send, done_recv,
):
    rep, faces, facing, partner = surroundings()
    group_count, k_blocks = out.shape[:2]
    batch_total, pages = values.shape[:2]
    r_groups = pages - 1
    inner = (group_count - 2 * REACH) // 2
    announce(faces, facing, partner)
    small = [
        pltpu.make_async_copy(table, table_scalars, small_sem.at[0]),
        pltpu.make_async_copy(sources, source_scalars, small_sem.at[1]),
    ]
    for copy in small:
        copy.start()

    def edge_at(which):
        return which * (group_count - REACH)

    def inner_at(which):
        return REACH + which * inner

    swaps = []

    def swap(at, size):
        index = len(swaps)
        rows_at = pl.ds(at, size)
        copy = remote(
            sent.at[rows_at], got.at[rows_at], swap_send.at[index], swap_recv.at[index], partner
        )
        copy.start()
        swaps.append(copy)

    def pack_edge(row):
        sent[row] = edge_total[(1 - rep) * REACH + row].astype(BF16)

    each(REACH, pack_edge)
    gather_round(faces)
    for step in range(REACH):
        swap(step, 1)

    blank = jnp.zeros(values.shape[2:], BF16)
    for scaled in (scaled_even, scaled_odd):
        scaled[r_groups] = blank
    terms[batch_total * r_groups] = jnp.zeros(terms.shape[1:], F32)
    for copy in small:
        copy.wait()

    def scale(b, scaled):
        row = factor[pl.ds(b, 1), :]
        for i in range(r_groups):
            scaled[i] = (values[b, i].astype(F32) * row).astype(BF16)

    def make_terms(b, scaled):
        for i in range(r_groups):
            code = b * r_groups + i
            for k in range(0, k_blocks, 2):
                columns = jnp.concatenate(
                    [scaled[table_scalars[k, code]], scaled[table_scalars[k + 1, code]]], axis=0
                )
                pair = lax.dot_general(
                    values[b, i], columns, (((1,), (1,)), ((), ())), preferred_element_type=F32
                )
                side = pair.shape[0]
                terms[code, k] = pair[:, :side]
                terms[code, k + 1] = pair[:, side:]

    def two_batches(step):
        scale(2 * step, scaled_even)
        scale(2 * step + 1, scaled_odd)
        make_terms(2 * step, scaled_even)
        make_terms(2 * step + 1, scaled_odd)

    early = 1
    each(early, two_batches)

    edges = []
    for step in range(REACH):
        swaps[step].wait_recv()
        edge_out[step] = (edge_total[rep * REACH + step] + got[step].astype(F32)).astype(BF16)
        edge = remote(edge_out.at[step], edge_in.at[step], edge_send.at[step], edge_recv.at[step], facing)
        edges.append(edge)

        @pl.when(faces)
        def _():
            edge.start()

    each(batch_total // 2 - early, lambda step: two_batches(step + early))

    def row_sum(row, k):
        held = terms[source_scalars[row, 0], k]
        for b in range(1, batch_total):
            held = held + terms[source_scalars[row, b], k]
        return held

    def pack(first, at, size):
        def step(row):
            for k in range(k_blocks):
                sent[at + row, k] = row_sum(first + row, k).astype(BF16)

        each(size, step)
        swap(at, size)

    pack(inner_at(1 - rep), 2 * REACH, inner // 2)
    pack(inner_at(1 - rep) + inner // 2, 2 * REACH + inner // 2, inner // 2)
    pack(edge_at(1 - rep), REACH, REACH)

    finals = []

    def hand_over(first, size):
        index = len(finals)
        rows_at = pl.ds(first, size)
        copy = remote(
            out.at[rows_at], out.at[rows_at], done_send.at[index], done_recv.at[index], partner
        )
        copy.start()
        finals.append(copy)

    for half in range(2):
        swaps[REACH + half].wait_recv()
        first = inner_at(rep) + half * (inner // 2)
        at = 2 * REACH + half * (inner // 2)

        def add_inner(row, first=first, at=at):
            for k in range(k_blocks):
                out[first + row, k] = (row_sum(first + row, k) + got[at + row, k].astype(F32)).astype(BF16)

        each(inner // 2, add_inner)
        hand_over(first, inner // 2)

    swaps[REACH + 2].wait_recv()

    def add_owned(row):
        for k in range(k_blocks):
            owned[row, k] = row_sum(edge_at(rep) + row, k) + got[REACH + row, k].astype(F32)

    each(REACH, add_owned)
    for step in range(REACH):
        row = edge_at(rep) + step

        @pl.when(faces)
        def _():
            edges[step].wait_recv()
            out[row] = (owned[step] + edge_in[step].astype(F32)).astype(BF16)

        @pl.when(jnp.logical_not(faces))
        def _():
            out[row] = owned[step].astype(BF16)

        hand_over(row, 1)

    @pl.when(faces)
    def _():
        for edge in edges:
            edge.wait_send()

    for copy in swaps:
        copy.wait_send()
    for copy in finals:
        copy.wait()


def reduced(edge_total, factor, fetched):
    _, values, _, _, table, sources = fetched
    group_count = sources.shape[0]
    k_blocks, side, _ = edge_total.shape[1:]
    batch_total, pages = values.shape[:2]
    half_rows = (group_count + 2 * REACH) // 2
    vector = pl.BlockSpec(memory_space=pltpu.VMEM)
    dma = pltpu.SemaphoreType.DMA
    return pl.pallas_call(
        reduce_kernel,
        out_shape=pltpu.VMEM((group_count, k_blocks, side, side), BF16),
        in_specs=[vector] * 5,
        out_specs=vector,
        scratch_shapes=[
            pltpu.SMEM(table.shape, jnp.int32),
            pltpu.SMEM(sources.shape, jnp.int32),
            pltpu.VMEM((batch_total * (pages - 1) + 1, k_blocks, side, side), F32),
            pltpu.VMEM((pages, side, side), BF16),
            pltpu.VMEM((pages, side, side), BF16),
            pltpu.VMEM((half_rows, k_blocks, side, side), BF16),
            pltpu.VMEM((half_rows, k_blocks, side, side), BF16),
            pltpu.VMEM((REACH, k_blocks, side, side), F32),
            pltpu.VMEM((REACH, k_blocks, side, side), BF16),
            pltpu.VMEM((REACH, k_blocks, side, side), BF16),
            dma((2,)),
            dma((REACH + 3,)),
            dma((REACH + 3,)),
            dma((REACH,)),
            dma((REACH,)),
            dma((REACH + 2,)),
            dma((REACH + 2,)),
        ],
        compiler_params=pltpu.CompilerParams(
            collective_id=1, has_side_effects=True, vmem_limit_bytes=40 * MIB
        ),
        name="reduce",
    )(in_vmem(edge_total), in_vmem(values), in_vmem(factor), in_vmem(table), in_vmem(sources))


def shards(density_blocks, neighbours, relevant, batch_count, basis_values, becke_weights):
    fetched = fetch_halo(relevant.T, neighbours.T, density_blocks, basis_values)
    edge_total, factor = edge_sums(batch_count, fetched, becke_weights, density_blocks.shape[0])
    return reduced(edge_total, factor, fetched)


def solution(mesh):
    placed = (
        P("grid", None, None, None),
        P("grid", None),
        P(("grid", "rep"), None),
        P(("grid", "rep")),
        P(("grid", "rep"), None, None, None),
        P(("grid", "rep"), None),
    )
    return jax.shard_map(
        shards, mesh=mesh, in_specs=placed, out_specs=P("grid", None, None, None), check_vma=False
    )
```

time: 50.3 us -> 45.7 us (0.909)
  the two profiles are of different devices: /device:TPU:3 before, /device:TPU:5 now
where the time goes in v2:
time: 45.7 us; the launch traced here: 45.6 us
  Pallas kernels  43 us (94%)
  local copies, waits for them, and re-layouts  1.84 us (4%)
  between operations  0.7 us (2%)
    pallas_call x1, Pallas kernels, reduced(): pl.pallas_call(reduce_kernel, out_shape=pltpu.VMEM((group_count, k_blocks...  21.5 us
    pallas_call x1, Pallas kernels, fetch_halo(): pl.pallas_call(halo_kernel, out_shape=(pltpu.VMEM((2 * REACH, k_blocks, s...  20.3 us
    unnamed x3, local copies, waits for them, and re-layouts  1.84 us
    pallas_call x1, Pallas kernels, edge_sums(): pl.pallas_call(functools.partial(edge_kernel, group_count), out_shape=(pl...  1.24 us

profile of v2, /device:TPU:5, one launch (start us, length us, event | category | flops | bytes accessed | tf_op | source)
XLA Modules:
  0.0 45.6 jit_solution(4279311478832290149)
XLA Ops:
  0.0 0.0 copy-start
  0.7 20.3 %halo.1 = (bf16[12,4,128,128]{3,2,1,0:T(8,128)(2,1)S(1)}, bf16[12,9,128,128]{3,2,1,0:T(8,128)(2,1)S(1)}, f32[12,4,128,128]{3,2,1,0:T(8,128)S(1)}, f32[12,8,128]{...) custom-call(s32[8,12]{1,0:T(8,128)} %bitcast.2, s32[4,28]{1,0:T(4,128)} %bitcast.3, ...), custom_call_target="tpu_custom_call" | custom-call | tf_op jit(solution)/shard_map/halo/pallas_call | solution.py:257
  21.0 0.0 copy-done
  21.0 1.2 %edges.1 = (f32[12,4,128,128]{3,2,1,0:T(8,128)S(1)}, f32[12,128]{1,0:T(8,128)S(1)}) custom-call(s32[1]{0:T(128)S(6)} %copy.11.live, s32[8,128]{1,0:T(8,128)S(1)} %get-tuple-element.13.table, bf16[12,128]{1,0:T(8,128)(2,1)S(1)} %copy-done, bf16[12,4,128,128]{3,2,1,0:T(8,128)(2,1)S(1)} %get-tuple-element.14.halo, ...), custom_call_target="tpu_custom_call", output_to_operand_aliasing={{0}: (6, {})} | custom-call | tf_op jit(solution)/shard_map/edges/pallas_call | solution.py:379
  22.2 21.5 %reduce.1 = bf16[28,4,128,128]{3,2,1,0:T(8,128)(2,1)S(1)} custom-call(f32[12,4,128,128]{3,2,1,0:T(8,128)S(1)} %get-tuple-element.18.edge_total, bf16[12,9,128,128]{3,2,1,0:T(8,128)(2,1)S(1)} %get-tuple-element.15.values, f32[12,128]{1,0:T(8,128)S(1)} %get-tuple-element.19.factor, s32[8,128]{1,0:T(8,128)S(1)} %get-tuple-element.13.table, ...), custom_call_target="tpu_custom_call" | custom-call | tf_op jit(solution)/shard_map/reduce/pallas_call | solution.py:569
  43.7 1.8 %copy.10 = bf16[28,4,128,128]{3,2,1,0:T(8,128)(2,1)} copy(bf16[28,4,128,128]{3,2,1,0:T(8,128)(2,1)S(1)} %reduce.1) | data formatting | bytes 7340032
Async XLA Ops:
  0.0 21.0 %copy-start = (bf16[12,128]{1,0:T(8,128)(2,1)S(1)}, bf16[12,128]{1,0:T(8,128)(2,1)}, u32[]{:S(2)}) copy-start(bf16[12,128]{1,0:T(8,128)(2,1)} %weights.1) | copy-start | bytes 9220
